TPU v7x, 256 devices: a whole 4x4x8 slice. The times are simulated.
256 devices in a mesh: rows: 64 (over y, z, core), cols: 4 (over x).
Axes of the slice: x: 4, y: 4, z: 8, core: 2. Of those that a mesh axis runs over, the one named last changes fastest.
Arguments:
- residual_block: float32 [524288, 64], P('rows', 'cols'), may hold values from -6 to 6
- basis: bfloat16 [524288, 64], P('rows', 'cols'), may hold values from -0.0078125 to 0.0078125
- fine_tiles: bfloat16 [4096, 4, 128, 128], P('rows')
- fine_index: int32 [4096, 4], P('rows'), may hold values from 0 to 4095, as said below
- mid_tiles: bfloat16 [512, 3, 128, 128], P('rows')
- fine_owner: int32 [524288], P('rows'), may hold values from 0 to 65535, as said below
- mid_owner: int32 [65536], P('rows'), may hold values from 0 to 8191, as said below
- coarse_inverse: float32 [8192, 8192], P('rows'), as said below
Outputs:
- directions: float32 [524288, 64], P('rows', 'cols')
- gram: float32 [64, 64], P(None, 'cols')
Inputs may be any that keep to these rules, and one draw needn't show every extreme that they name: `fine_index`: slot 0 of block row g names g itself; every block named in a block row of partition p (block rows p*64 to p*64 + 63) belongs to partition p - 1, p or p + 1. `fine_owner`: the fine vertices of partition p map to level-one rows p*1024 to p*1024 + 1023; every level-one row receives exactly 8 vertices. `mid_owner`: the level-one rows of partitions 2q and 2q + 1 map to level-two rows 2q*128 to 2q*128 + 2*128 - 1; every level-two row receives exactly 8 level-one rows. coarse_inverse is symmetric.
All inputs are finite; a program needn't handle non-finite values.
Results may differ from a plain program's by a relative error of at most 0.013.
Values may be sent and summed in bfloat16 or wider, within the bound.
A program may use at most 64 MiB of HBM per device.

v0:
```python
import jax
import jax.numpy as jnp
from jax import lax
from jax.sharding import PartitionSpec as P

DAMPING = 0.6666666666666666


def with_halo(array, sides, width):
    for axis, dim in sides:
        peers, length = (lax.axis_size(axis), array.shape[dim])
        up = [(i, (i + 1) % peers) for i in range(peers - 1)]
        down = [(j, i) for i, j in up]
        last = lax.slice_in_dim(array, length - width, length, axis=dim)
        leading = lax.slice_in_dim(array, 0, width, axis=dim)
        before = lax.ppermute(last, axis, up)
        after = lax.ppermute(leading, axis, down)
        array = jnp.concatenate([before, array, after], axis=dim)
    return array


def swapped(value, axis, apart):
    mask = 2**apart
    pairs = [(source, source ^ mask) for source in range(lax.axis_size(axis))]
    return lax.ppermute(value, axis, pairs)


def fine_apply(vector, matrix, window_index):
    extent = matrix.shape[2]
    packed = vector.astype(jnp.bfloat16).reshape(-1, extent, vector.shape[1])
    window = with_halo(packed, (("rows", 0),), packed.shape[0])
    picked = window[window_index]
    product = jnp.einsum("bkij,bkjc->bic", matrix, picked, preferred_element_type=jnp.float32)
    return product.reshape(vector.shape)


def mid_apply(vector, matrix):
    blocks = matrix.shape[0]
    extent = matrix.shape[2]
    packed = vector.astype(jnp.bfloat16).reshape(blocks, extent, vector.shape[1])
    window = with_halo(packed, (("rows", 0),), 1)
    product = jnp.einsum(
        "bij,bjc->bic", matrix[:, 0], window[:-2], preferred_element_type=jnp.float32
    )
    product = product + jnp.einsum(
        "bij,bjc->bic", matrix[:, 1], window[1:-1], preferred_element_type=jnp.float32
    )
    product = product + jnp.einsum(
        "bij,bjc->bic", matrix[:, 2], window[2:], preferred_element_type=jnp.float32
    )
    return product.reshape(vector.shape)


def on_device(
    residual_block, basis, fine_tiles, fine_index, mid_tiles, fine_owner, mid_owner, coarse_inverse
):
    device = lax.axis_index("rows")
    blocks = fine_tiles.shape[0]
    mid_count = mid_tiles.shape[0] * mid_tiles.shape[2]
    coarse_count = coarse_inverse.shape[0]
    col_width = residual_block.shape[1]
    parity = device % 2
    window_index = fine_index - (device - 1) * blocks
    fine_local = fine_owner - device * mid_count
    mid_local = mid_owner - (device - parity) * coarse_count
    fine_inv = 1.0 / jnp.diagonal(fine_tiles[:, 0], axis1=1, axis2=2).astype(jnp.float32).reshape(
        -1, 1
    )
    mid_inv = 1.0 / jnp.diagonal(mid_tiles[:, 1], axis1=1, axis2=2).astype(jnp.float32).reshape(
        -1, 1
    )
    fine_x = DAMPING * fine_inv * residual_block
    fine_x = fine_x + DAMPING * fine_inv * (
        residual_block - fine_apply(fine_x, fine_tiles, window_index)
    )
    fine_res = residual_block - fine_apply(fine_x, fine_tiles, window_index)
    partial_mid = jax.ops.segment_sum(fine_res, fine_local, num_segments=mid_count)
    mid_x = DAMPING * mid_inv * partial_mid
    mid_x = mid_x + DAMPING * mid_inv * (partial_mid - mid_apply(mid_x, mid_tiles))
    mid_res = partial_mid - mid_apply(mid_x, mid_tiles)
    partial_value = jax.ops.segment_sum(mid_res, mid_local, num_segments=2 * coarse_count)
    halves = partial_value.reshape(2, coarse_count, col_width)
    own_half = jnp.where(parity == 0, halves[0], halves[1])
    other_half = jnp.where(parity == 0, halves[1], halves[0])
    coarse_rhs = own_half + swapped(other_half, "rows", 0)
    coarse_fix = jnp.dot(
        coarse_inverse,
        lax.all_gather(coarse_rhs, "rows", axis=0, tiled=True),
        precision=lax.Precision.HIGHEST,
        preferred_element_type=jnp.float32,
    )
    partner_fix = swapped(coarse_fix, "rows", 0)
    pair_values = jnp.where(
        parity == 0,
        jnp.concatenate([coarse_fix, partner_fix], axis=0),
        jnp.concatenate([partner_fix, coarse_fix], axis=0),
    )
    mid_x = mid_x + pair_values[mid_local]
    mid_x = mid_x + DAMPING * mid_inv * (partial_mid - mid_apply(mid_x, mid_tiles))
    fine_x = fine_x + mid_x[fine_local]
    finished = fine_x + DAMPING * fine_inv * (
        residual_block - fine_apply(fine_x, fine_tiles, window_index)
    )
    rounded = finished.astype(jnp.bfloat16)
    partial_gram = lax.dot_general(
        lax.all_gather(basis, "cols", axis=1, tiled=True),
        rounded,
        (((0,), (0,)), ((), ())),
        preferred_element_type=jnp.float32,
    )
    gram = lax.psum(partial_gram, "rows")
    return (finished, gram)


def solution(mesh):
    in_specs = (
        P("rows", "cols"),
        P("rows", "cols"),
        P("rows", None, None, None),
        P("rows", None),
        P("rows", None, None, None),
        P("rows"),
        P("rows"),
        P("rows", None),
    )
    out_specs = (P("rows", "cols"), P(None, "cols"))
    return jax.shard_map(
        on_device, mesh=mesh, in_specs=in_specs, out_specs=out_specs, check_vma=False
    )
```

profile of v0, /device:TPU:4, one launch (start us, length us, event | category | flops | bytes accessed | tf_op | source)
XLA Modules:
  0.0 407.9 jit_solution(2754003155523653004)
XLA Ops:
  8.8 3.9 copy.204
  12.7 1.9 gather_fusion
  19.1 3.1 copy.166
  25.2 5.7 %convolution_bitcast_fusion.2 = f32[64,2,8,128]{3,2,1,0:T(8,128)S(1)} fusion(bf16[64,4,128,16]{2,3,1,0:T(8,128)(2,1)S(1)} %bitcast.177, bf16[64,4,128,128]{3,2,1,0:T(8,128)(2,1)} %param.10), kind=kOutput, calls=%fused_computation.11 | convolution fusion | flops 134217728 | bytes 9961472 | tf_op jit(solution)/shard_map/bkij,bkjc->bic/dot_general | solution.py:33
  31.0 4.7 %collective-permute-start.2 = (bf16[64,128,16]{1,2,0:T(8,128)(2,1)S(1)}, bf16[64,128,16]{1,2,0:T(8,128)(2,1)S(1)}, u32[]{:S(2)}, u32[]{:S(2)}) collective-permute-start(bf16[64,128,16]{1,2,0:T(8,128)(2,1)S(1)} %copy_bitcast_fusion.1), channel_id=1, source_target_pairs={{0,4},{4,8},{8,12},{12,16},{16,20},{20,24},{24,28},{28,32},{32,36}... | collective-permute-start | bytes 786440 | tf_op jit(solution)/shard_map/ppermute | solution.py:16
  37.1 3.3 collective-permute-done.3
  41.3 5.7 %convolution_bitcast_fusion.1 = f32[64,2,8,128]{3,2,1,0:T(8,128)S(1)} fusion(bf16[64,4,128,16]{2,3,1,0:T(8,128)(2,1)S(1)} %bitcast.178, bf16[64,4,128,128]{3,2,1,0:T(8,128)(2,1)} %param.10), kind=kOutput, calls=%fused_computation.10 | convolution fusion | flops 134217728 | bytes 9961472 | tf_op jit(solution)/shard_map/bkij,bkjc->bic/dot_general | solution.py:33
  47.1 2.6 copy.172
  49.7 44.4 %scatter_custom_fusion = f32[1024,16]{1,0:T(8,128)S(1)} fusion(s32[8192]{0:T(1024)S(1)} %get-tuple-element.11, f32[8192,16]{1,0:T(8,128)} %copy.172, f32[]{:T(128)} %constant.25.clone.1), kind=kCustom, calls=%fused_computation.51 | custom fusion | flops 131072 | bytes 66048 | tf_op jit(solution)/shard_map/scatter-add | solution.py:77
  95.9 7.3 %collective-permute-start.4 = (bf16[1,128,16]{1,2,0:T(8,128)(2,1)S(1)}, bf16[1,128,16]{1,2,0:T(8,128)(2,1)S(1)}, u32[]{:S(2)}, u32[]{:S(2)}) collective-permute-start(bf16[1,128,16]{1,2,0:T(8,128)(2,1)S(1)} %get-tuple-element.18), channel_id=1, source_target_pairs={{0,4},{4,8},{8,12},{12,16},{16,20},{20,24},{24,28},{28,32},{32,36}... | collective-permute-start | bytes 12296 | tf_op jit(solution)/shard_map/ppermute | solution.py:16
  105.8 4.2 %collective-permute-start.6 = (bf16[1,128,16]{1,2,0:T(8,128)(2,1)S(1)}, bf16[1,128,16]{1,2,0:T(8,128)(2,1)S(1)}, u32[]{:S(2)}, u32[]{:S(2)}) collective-permute-start(bf16[1,128,16]{1,2,0:T(8,128)(2,1)S(1)} %get-tuple-element.16), channel_id=1, source_target_pairs={{0,4},{4,8},{8,12},{12,16},{16,20},{20,24},{24,28},{28,32},{32,36}... | collective-permute-start | bytes 12296 | tf_op jit(solution)/shard_map/ppermute | solution.py:16
  112.2 6.4 %scatter_custom_fusion.1 = f32[256,16]{1,0:T(8,128)S(1)} fusion(s32[1024]{0:T(1024)S(1)} %get-tuple-element.13, f32[1024,16]{1,0:T(8,128)} %bitcast_subtract_fusion.3, f32[]{:T(128)} %constant.25.clone.1), kind=kCustom, calls=%fused_computation.70 | custom fusion | flops 16384 | bytes 16896 | tf_op jit(solution)/shard_map/scatter-add | solution.py:81
  118.6 2.5 collective-permute-start.8
  122.0 65.2 %all_gather.6 = f32[8192,16]{1,0:T(8,128)S(1)} all-gather(f32[128,16]{1,0:T(8,128)S(1)} %select_add_fusion), channel_id=1, replica_groups=mesh['rows'=64,'cols'=4] {'rows'}, dimensions={0}, use_global_device_ids=true | all-gather | bytes 532480 | tf_op jit(solution)/shard_map/all_gather | solution.py:88
  187.2 6.6 %convolution_bitcast_fusion.4 = f32[128,16]{0,1:T(8,128)S(1)} fusion(f32[8192,16]{1,0:T(8,128)S(1)} %all_gather.6, f32[128,8192]{1,0:T(8,128)S(1)} %copy-done.2), kind=kOutput, calls=%fused_computation.22 | convolution fusion | flops 201326592 | bytes 4726784 | tf_op jit(solution)/shard_map/dot_general | solution.py:86
  195.1 2.8 gather_fusion.4
  199.7 3.0 collective-permute-start.10
  204.0 27.9 %gather_fusion.5 = f32[8192,16]{1,0:T(8,128)} fusion(f32[1024,16]{1,0:T(8,128)S(1)} %copy.193, s32[8192]{0:T(1024)S(1)} %get-tuple-element.10), kind=kCustom, calls=%fused_computation.5 | custom fusion | bytes 1081344 | tf_op jit(solution)/shard_map/gather | solution.py:100
  231.9 2.8 copy.194
  234.8 3.4 collective-permute-start.12
  239.6 3.9 collective-permute-done.13
  244.4 5.7 %convolution_bitcast_fusion = f32[64,2,8,128]{3,2,1,0:T(8,128)S(1)} fusion(bf16[64,4,128,16]{2,3,1,0:T(8,128)(2,1)S(1)} %bitcast.176, bf16[64,4,128,128]{3,2,1,0:T(8,128)(2,1)} %param.10), kind=kOutput, calls=%fused_computation.9 | convolution fusion | flops 134217728 | bytes 9961472 | tf_op jit(solution)/shard_map/bkij,bkjc->bic/dot_general | solution.py:33
  250.3 18.4 %all-gather.2.cloned.1.call-done = bf16[8192,64]{0,1:T(8,128)(2,1)} async-done(((bf16[8192,16]{0,1:T(8,128)(2,1)}), bf16[8192,64]{0,1:T(8,128)(2,1)}) %all-gather.2.cloned.1.call-update) | async-done | bytes 1048592 | tf_op jit(solution)/shard_map/all_gather | solution.py:106
  270.3 130.8 %psum.7 = f32[64,16]{0,1:T(8,128)} all-reduce(f32[64,16]{0,1:T(8,128)S(1)} %convolution_bitcast_fusion.3), channel_id=1, replica_groups=mesh['rows'=64,'cols'=4] {'rows'}, use_global_device_ids=true, to_apply=%region_2.3 | all-reduce | flops 1024 | bytes 8192 | tf_op jit(solution)/shard_map/psum | solution.py:111
  (91 shorter events, 27.2 us)
Async XLA Ops:
  7.2 1.6 slice-start
  7.2 261.5 %all-gather.2.cloned.1.call-start = ((), (), s32[]{:S(2)}) async-start(), calls=%async_computation | async-start | bytes 1310720 | tf_op jit(solution)/shard_map/all_gather | solution.py:106
  8.8 6.0 %copy-start = (f32[8192,16]{0,1:T(8,128)S(1)}, f32[8192,16]{0,1:T(8,128)}, u32[]{:S(2)}) copy-start(f32[8192,16]{0,1:T(8,128)} %param.8) | copy-start | bytes 1572868
  8.8 9.1 %copy-start.6 = (s32[64,4]{0,1:T(4,128)S(1)}, s32[64,4]{0,1:T(4,128)}, u32[]{:S(2)}) copy-start(s32[64,4]{0,1:T(4,128)} %param.11) | copy-start | bytes 3076
  12.7 11.5 %copy-start.5 = (s32[1024]{0:T(1024)S(1)}, s32[1024]{0:T(1024)}, u32[]{:S(2)}) copy-start(s32[1024]{0:T(1024)} %param.14) | copy-start | bytes 12292
  14.8 9.4 %collective-permute-start = (bf16[64,128,16]{1,2,0:T(8,128)(2,1)S(1)}, bf16[64,128,16]{1,2,0:T(8,128)(2,1)S(1)}, u32[]{:S(2)}, u32[]{:S(2)}) collective-permute-start(bf16[64,128,16]{1,2,0:T(8,128)(2,1)S(1)} %copy_bitcast_fusion.2), channel_id=1, source_target_pairs={{0,4},{4,8},{8,12},{12,16},{16,20},{20,24},{24,28},{28,32},{32,36}... | collective-permute-start | bytes 786440 | tf_op jit(solution)/shard_map/ppermute | solution.py:16
  16.5 7.7 %collective-permute-start.1 = (bf16[64,128,16]{1,2,0:T(8,128)(2,1)S(1)}, bf16[64,128,16]{1,2,0:T(8,128)(2,1)S(1)}, u32[]{:S(2)}, u32[]{:S(2)}) collective-permute-start(bf16[64,128,16]{1,2,0:T(8,128)(2,1)S(1)} %copy_bitcast_fusion.2), channel_id=1, source_target_pairs={{4,0},{8,4},{12,8},{16,12},{20,16},{24,20},{28,24},{32,28},{36,32}... | collective-permute-start | bytes 786440 | tf_op jit(solution)/shard_map/ppermute | solution.py:17
  25.2 11.9 %copy-start.4 = (s32[8192]{0:T(1024)S(1)}, s32[8192]{0:T(1024)}, u32[]{:S(2)}) copy-start(s32[8192]{0:T(1024)} %param.13) | copy-start | bytes 98308
  31.0 6.1 %collective-permute-start.2 = (bf16[64,128,16]{1,2,0:T(8,128)(2,1)S(1)}, bf16[64,128,16]{1,2,0:T(8,128)(2,1)S(1)}, u32[]{:S(2)}, u32[]{:S(2)}) collective-permute-start(bf16[64,128,16]{1,2,0:T(8,128)(2,1)S(1)} %copy_bitcast_fusion.1), channel_id=1, source_target_pairs={{0,4},{4,8},{8,12},{12,16},{16,20},{20,24},{24,28},{28,32},{32,36}... | collective-permute-start | bytes 786440 | tf_op jit(solution)/shard_map/ppermute | solution.py:16
  35.7 4.7 %collective-permute-start.3 = (bf16[64,128,16]{1,2,0:T(8,128)(2,1)S(1)}, bf16[64,128,16]{1,2,0:T(8,128)(2,1)S(1)}, u32[]{:S(2)}, u32[]{:S(2)}) collective-permute-start(bf16[64,128,16]{1,2,0:T(8,128)(2,1)S(1)} %copy_bitcast_fusion.1), channel_id=1, source_target_pairs={{4,0},{8,4},{12,8},{16,12},{20,16},{24,20},{28,24},{32,28},{36,32}... | collective-permute-start | bytes 786440 | tf_op jit(solution)/shard_map/ppermute | solution.py:17
  47.0 47.3 %copy-start.1 = (bf16[8,3,128,128]{3,2,1,0:T(8,128)(2,1)S(1)}, bf16[8,3,128,128]{3,2,1,0:T(8,128)(2,1)}, u32[]{:S(2)}) copy-start(bf16[8,3,128,128]{3,2,1,0:T(8,128)(2,1)} %param.12) | copy-start | bytes 2359300
  94.6 8.6 %collective-permute-start.5 = (bf16[1,128,16]{1,2,0:T(8,128)(2,1)S(1)}, bf16[1,128,16]{1,2,0:T(8,128)(2,1)S(1)}, u32[]{:S(2)}, u32[]{:S(2)}) collective-permute-start(bf16[1,128,16]{1,2,0:T(8,128)(2,1)S(1)} %get-tuple-element.19), channel_id=1, source_target_pairs={{4,0},{8,4},{12,8},{16,12},{20,16},{24,20},{28,24},{32,28},{36,32}... | collective-permute-start | bytes 12296 | tf_op jit(solution)/shard_map/ppermute | solution.py:17
  95.9 8.1 %collective-permute-start.4 = (bf16[1,128,16]{1,2,0:T(8,128)(2,1)S(1)}, bf16[1,128,16]{1,2,0:T(8,128)(2,1)S(1)}, u32[]{:S(2)}, u32[]{:S(2)}) collective-permute-start(bf16[1,128,16]{1,2,0:T(8,128)(2,1)S(1)} %get-tuple-element.18), channel_id=1, source_target_pairs={{0,4},{4,8},{8,12},{12,16},{16,20},{20,24},{24,28},{28,32},{32,36}... | collective-permute-start | bytes 12296 | tf_op jit(solution)/shard_map/ppermute | solution.py:16
  104.5 5.5 %collective-permute-start.7 = (bf16[1,128,16]{1,2,0:T(8,128)(2,1)S(1)}, bf16[1,128,16]{1,2,0:T(8,128)(2,1)S(1)}, u32[]{:S(2)}, u32[]{:S(2)}) collective-permute-start(bf16[1,128,16]{1,2,0:T(8,128)(2,1)S(1)} %get-tuple-element.17), channel_id=1, source_target_pairs={{4,0},{8,4},{12,8},{16,12},{20,16},{24,20},{28,24},{32,28},{36,32}... | collective-permute-start | bytes 12296 | tf_op jit(solution)/shard_map/ppermute | solution.py:17
  105.8 5.0 %collective-permute-start.6 = (bf16[1,128,16]{1,2,0:T(8,128)(2,1)S(1)}, bf16[1,128,16]{1,2,0:T(8,128)(2,1)S(1)}, u32[]{:S(2)}, u32[]{:S(2)}) collective-permute-start(bf16[1,128,16]{1,2,0:T(8,128)(2,1)S(1)} %get-tuple-element.16), channel_id=1, source_target_pairs={{0,4},{4,8},{8,12},{12,16},{16,20},{20,24},{24,28},{28,32},{32,36}... | collective-permute-start | bytes 12296 | tf_op jit(solution)/shard_map/ppermute | solution.py:16
  118.6 68.6 %copy-start.2 = (f32[128,8192]{1,0:T(8,128)S(1)}, f32[128,8192]{1,0:T(8,128)}, u32[]{:S(2)}) copy-start(f32[128,8192]{1,0:T(8,128)} %param.15) | copy-start | bytes 12582916
  118.6 3.4 collective-permute-start.8
  193.8 1.2 collective-permute-start.9
  198.4 4.4 %collective-permute-start.11 = (bf16[1,128,16]{1,2,0:T(8,128)(2,1)S(1)}, bf16[1,128,16]{1,2,0:T(8,128)(2,1)S(1)}, u32[]{:S(2)}, u32[]{:S(2)}) collective-permute-start(bf16[1,128,16]{1,2,0:T(8,128)(2,1)S(1)} %get-tuple-element.15), channel_id=1, source_target_pairs={{4,0},{8,4},{12,8},{16,12},{20,16},{24,20},{28,24},{32,28},{36,32}... | collective-permute-start | bytes 12296 | tf_op jit(solution)/shard_map/ppermute | solution.py:17
  199.7 3.8 collective-permute-start.10
  234.8 4.8 %collective-permute-start.12 = (bf16[64,128,16]{1,2,0:T(8,128)(2,1)S(1)}, bf16[64,128,16]{1,2,0:T(8,128)(2,1)S(1)}, u32[]{:S(2)}, u32[]{:S(2)}) collective-permute-start(bf16[64,128,16]{1,2,0:T(8,128)(2,1)S(1)} %copy_bitcast_fusion), channel_id=1, source_target_pairs={{0,4},{4,8},{8,12},{12,16},{16,20},{20,24},{24,28},{28,32},{32,36}... | collective-permute-start | bytes 786440 | tf_op jit(solution)/shard_map/ppermute | solution.py:16
  238.3 5.2 %collective-permute-start.13 = (bf16[64,128,16]{1,2,0:T(8,128)(2,1)S(1)}, bf16[64,128,16]{1,2,0:T(8,128)(2,1)S(1)}, u32[]{:S(2)}, u32[]{:S(2)}) collective-permute-start(bf16[64,128,16]{1,2,0:T(8,128)(2,1)S(1)} %copy_bitcast_fusion), channel_id=1, source_target_pairs={{4,0},{8,4},{12,8},{16,12},{20,16},{24,20},{28,24},{32,28},{36,32}... | collective-permute-start | bytes 786440 | tf_op jit(solution)/shard_map/ppermute | solution.py:17
  250.3 150.8 %copy-start.3 = (f32[8192,16]{0,1:T(8,128)}, f32[8192,16]{0,1:T(8,128)S(1)}, u32[]{:S(2)}) copy-start(f32[8192,16]{0,1:T(8,128)S(1)} %fusion.7) | copy-start | bytes 1572868
Sparse Core Ops, SparseCore 0:
  239.7 28.9 all-gather.1
where the time goes:
time: 409 us; the launch traced here: 408 us
  blocking collectives  196 us (48%)
  local copies, waits for them, and re-layouts  53.3 us (13%)
  other arithmetic  52.8 us (13%)
  starting transfers between devices  35.1 us (9%)
  waiting for transfers between devices  29 us (7%)
  matrix products  27.3 us (7%)
  between operations  14.5 us (4%)
    psum x1, blocking collectives, on_device(): gram = lax.psum(partial_gram, 'rows')  131 us
    all_gather x1, blocking collectives, on_device(): lax.all_gather(coarse_rhs, 'rows', axis=0, tiled=True)  65.2 us
    scatter-add x1, other arithmetic, on_device(): jax.ops.segment_sum(fine_res, fine_local, num_segments=mid_count)  44.4 us
    gather x2, local copies, waits for them, and re-layouts, on_device(): fine_x = fine_x + mid_x[fine_local]  30.7 us
    ppermute x6, starting transfers between devices, with_halo(): before = lax.ppermute(last, axis, up)  24.4 us
    all_gather x1, waiting for transfers between devices, on_device(): lax.all_gather(basis, 'cols', axis=1, tiled=True)  18.4 us
    dot_general x3, matrix products, fine_apply(): jnp.einsum('bkij,bkjc->bic', matrix, picked, preferred_element_type=jnp.f...  17 us
  transfers between devices with their start and end apart: 15, of which 8 were waited for; matrix products, arithmetic and copies ran while one was open for 3% of the time, Pallas kernels for 0%

commit v1 on v0

--- a/solution.py
+++ b/solution.py
@@ -108,7 +108,7 @@
         (((0,), (0,)), ((), ())),
         preferred_element_type=jnp.float32,
     )
-    gram = lax.psum(partial_gram, "rows")
+    gram = jnp.sum(lax.all_gather(partial_gram, "rows"), axis=0)
     return (finished, gram)
 
 

time: 409 us -> 332 us (0.81)
  blocking collectives: 196 us -> 116 us
    psum x1 -> x0, blocking collectives: 131 us -> none  [on_device(): gram = lax.psum(partial_gram, 'rows')]
    all_gather x0 -> x1, blocking collectives: none -> 51.1 us  [on_device(): gram = jnp.sum(lax.all_gather(partial_gram, 'rows'), axis=0)]
  transfers between devices with their start and end apart: 15 -> 15, of which waited for: 8 -> 8; matrix products, arithmetic and copies ran while one was open for 3% -> 4% of each run, Pallas kernels for 0% -> 0%
where the time goes in v1:
time: 332 us; the launch traced here: 329 us
  blocking collectives  116 us (35%)
  other arithmetic  53.5 us (16%)
  local copies, waits for them, and re-layouts  53.3 us (16%)
  starting transfers between devices  35.3 us (11%)
  waiting for transfers between devices  29 us (9%)
  matrix products  27.3 us (8%)
  between operations  14.5 us (4%)
    all_gather x1, blocking collectives, on_device(): lax.all_gather(coarse_rhs, 'rows', axis=0, tiled=True)  65.2 us
    all_gather x1, blocking collectives, on_device(): gram = jnp.sum(lax.all_gather(partial_gram, 'rows'), axis=0)  51.1 us
    scatter-add x1, other arithmetic, on_device(): jax.ops.segment_sum(fine_res, fine_local, num_segments=mid_count)  44.4 us
    gather x2, local copies, waits for them, and re-layouts, on_device(): fine_x = fine_x + mid_x[fine_local]  30.7 us
    ppermute x6, starting transfers between devices, with_halo(): before = lax.ppermute(last, axis, up)  24.4 us
    all_gather x1, waiting for transfers between devices, on_device(): lax.all_gather(basis, 'cols', axis=1, tiled=True)  18.6 us
    dot_general x3, matrix products, fine_apply(): jnp.einsum('bkij,bkjc->bic', matrix, picked, preferred_element_type=jnp.f...  17 us
    ppermute x6, starting transfers between devices, with_halo(): after = lax.ppermute(leading, axis, down)  8 us
  transfers between devices with their start and end apart: 15, of which 8 were waited for; matrix products, arithmetic and copies ran while one was open for 4% of the time, Pallas kernels for 0%

profile of v1, /device:TPU:4, one launch (start us, length us, event | category | flops | bytes accessed | tf_op | source)
XLA Modules:
  0.0 329.1 jit_solution(10381056839730479344)
XLA Ops:
  8.8 3.9 %copy.204 = bf16[64,1,128,128]{0,3,2,1:T(8,128)(2,1)} copy(bf16[64,1,128,128]{3,2,1,0:T(8,128)(2,1)S(1)} %slice-done) | data formatting | bytes 4194304
  12.7 1.9 gather_fusion
  19.1 3.1 copy.166
  25.2 5.7 %convolution_bitcast_fusion.2 = f32[64,2,8,128]{3,2,1,0:T(8,128)S(1)} fusion(bf16[64,4,128,16]{2,3,1,0:T(8,128)(2,1)S(1)} %bitcast.179, bf16[64,4,128,128]{3,2,1,0:T(8,128)(2,1)} %param.10), kind=kOutput, calls=%fused_computation.11 | convolution fusion | flops 134217728 | bytes 9961472 | tf_op jit(solution)/shard_map/bkij,bkjc->bic/dot_general | solution.py:33
  31.0 4.7 %collective-permute-start.2 = (bf16[64,128,16]{1,2,0:T(8,128)(2,1)S(1)}, bf16[64,128,16]{1,2,0:T(8,128)(2,1)S(1)}, u32[]{:S(2)}, u32[]{:S(2)}) collective-permute-start(bf16[64,128,16]{1,2,0:T(8,128)(2,1)S(1)} %copy_bitcast_fusion.1), channel_id=1, source_target_pairs={{0,4},{4,8},{8,12},{12,16},{16,20},{20,24},{24,28},{28,32},{32,36}... | collective-permute-start | bytes 786440 | tf_op jit(solution)/shard_map/ppermute | solution.py:16
  37.1 3.3 %collective-permute-done.3 = bf16[64,128,16]{1,2,0:T(8,128)(2,1)S(1)} collective-permute-done((bf16[64,128,16]{1,2,0:T(8,128)(2,1)S(1)}, bf16[64,128,16]{1,2,0:T(8,128)(2,1)S(1)}, u32[]{:S(2)}, u32[]{:S(2)}) %collective-permute-start.3) | collective-permute-done | bytes 262176 | tf_op jit(solution)/shard_map/ppermute | solution.py:17
  41.3 5.7 %convolution_bitcast_fusion.1 = f32[64,2,8,128]{3,2,1,0:T(8,128)S(1)} fusion(bf16[64,4,128,16]{2,3,1,0:T(8,128)(2,1)S(1)} %bitcast.180, bf16[64,4,128,128]{3,2,1,0:T(8,128)(2,1)} %param.10), kind=kOutput, calls=%fused_computation.10 | convolution fusion | flops 134217728 | bytes 9961472 | tf_op jit(solution)/shard_map/bkij,bkjc->bic/dot_general | solution.py:33
  47.1 2.6 copy.172
  49.7 44.4 %scatter_custom_fusion = f32[1024,16]{1,0:T(8,128)S(1)} fusion(s32[8192]{0:T(1024)S(1)} %get-tuple-element.11, f32[8192,16]{1,0:T(8,128)} %copy.172, f32[]{:T(128)} %constant.25.clone.1), kind=kCustom, calls=%fused_computation.51 | custom fusion | flops 131072 | bytes 66048 | tf_op jit(solution)/shard_map/scatter-add | solution.py:77
  95.9 7.3 %collective-permute-start.4 = (bf16[1,128,16]{1,2,0:T(8,128)(2,1)S(1)}, bf16[1,128,16]{1,2,0:T(8,128)(2,1)S(1)}, u32[]{:S(2)}, u32[]{:S(2)}) collective-permute-start(bf16[1,128,16]{1,2,0:T(8,128)(2,1)S(1)} %get-tuple-element.18), channel_id=1, source_target_pairs={{0,4},{4,8},{8,12},{12,16},{16,20},{20,24},{24,28},{28,32},{32,36}... | collective-permute-start | bytes 12296 | tf_op jit(solution)/shard_map/ppermute | solution.py:16
  105.8 4.2 %collective-permute-start.6 = (bf16[1,128,16]{1,2,0:T(8,128)(2,1)S(1)}, bf16[1,128,16]{1,2,0:T(8,128)(2,1)S(1)}, u32[]{:S(2)}, u32[]{:S(2)}) collective-permute-start(bf16[1,128,16]{1,2,0:T(8,128)(2,1)S(1)} %get-tuple-element.16), channel_id=1, source_target_pairs={{0,4},{4,8},{8,12},{12,16},{16,20},{20,24},{24,28},{28,32},{32,36}... | collective-permute-start | bytes 12296 | tf_op jit(solution)/shard_map/ppermute | solution.py:16
  112.2 6.4 %scatter_custom_fusion.1 = f32[256,16]{1,0:T(8,128)S(1)} fusion(s32[1024]{0:T(1024)S(1)} %get-tuple-element.13, f32[1024,16]{1,0:T(8,128)} %bitcast_subtract_fusion.3, f32[]{:T(128)} %constant.25.clone.1), kind=kCustom, calls=%fused_computation.70 | custom fusion | flops 16384 | bytes 16896 | tf_op jit(solution)/shard_map/scatter-add | solution.py:81
  118.6 2.5 collective-permute-start.8
  122.0 65.2 %all_gather.12 = f32[8192,16]{1,0:T(8,128)S(1)} all-gather(f32[128,16]{1,0:T(8,128)S(1)} %select_add_fusion), channel_id=1, replica_groups=mesh['rows'=64,'cols'=4] {'rows'}, dimensions={0}, use_global_device_ids=true | all-gather | bytes 532480 | tf_op jit(solution)/shard_map/all_gather | solution.py:88
  187.2 6.6 %convolution_bitcast_fusion.4 = f32[128,16]{0,1:T(8,128)S(1)} fusion(f32[8192,16]{1,0:T(8,128)S(1)} %all_gather.12, f32[128,8192]{1,0:T(8,128)S(1)} %copy-done.2), kind=kOutput, calls=%fused_computation.22 | convolution fusion | flops 201326592 | bytes 4726784 | tf_op jit(solution)/shard_map/dot_general | solution.py:86
  195.1 2.8 gather_fusion.4
  199.7 3.0 collective-permute-start.10
  204.0 27.9 %gather_fusion.5 = f32[8192,16]{1,0:T(8,128)} fusion(f32[1024,16]{1,0:T(8,128)S(1)} %copy.193, s32[8192]{0:T(1024)S(1)} %get-tuple-element.10), kind=kCustom, calls=%fused_computation.5 | custom fusion | bytes 1081344 | tf_op jit(solution)/shard_map/gather | solution.py:100
  231.9 2.8 copy.194
  234.8 3.4 %collective-permute-start.12 = (bf16[64,128,16]{1,2,0:T(8,128)(2,1)S(1)}, bf16[64,128,16]{1,2,0:T(8,128)(2,1)S(1)}, u32[]{:S(2)}, u32[]{:S(2)}) collective-permute-start(bf16[64,128,16]{1,2,0:T(8,128)(2,1)S(1)} %copy_bitcast_fusion), channel_id=1, source_target_pairs={{0,4},{4,8},{8,12},{12,16},{16,20},{20,24},{24,28},{28,32},{32,36}... | collective-permute-start | bytes 786440 | tf_op jit(solution)/shard_map/ppermute | solution.py:16
  239.8 3.6 %collective-permute-done.13 = bf16[64,128,16]{1,2,0:T(8,128)(2,1)S(1)} collective-permute-done((bf16[64,128,16]{1,2,0:T(8,128)(2,1)S(1)}, bf16[64,128,16]{1,2,0:T(8,128)(2,1)S(1)}, u32[]{:S(2)}, u32[]{:S(2)}) %collective-permute-start.13) | collective-permute-done | bytes 262176 | tf_op jit(solution)/shard_map/ppermute | solution.py:17
  244.4 5.7 %convolution_bitcast_fusion = f32[64,2,8,128]{3,2,1,0:T(8,128)S(1)} fusion(bf16[64,4,128,16]{2,3,1,0:T(8,128)(2,1)S(1)} %bitcast.178, bf16[64,4,128,128]{3,2,1,0:T(8,128)(2,1)} %param.10), kind=kOutput, calls=%fused_computation.9 | convolution fusion | flops 134217728 | bytes 9961472 | tf_op jit(solution)/shard_map/bkij,bkjc->bic/dot_general | solution.py:33
  250.3 18.6 %all-gather.4.cloned.1.call-done = bf16[8192,64]{0,1:T(8,128)(2,1)} async-done(((bf16[8192,16]{0,1:T(8,128)(2,1)}), bf16[8192,64]{0,1:T(8,128)(2,1)}) %all-gather.4.cloned.1.call-update) | async-done | bytes 1048592 | tf_op jit(solution)/shard_map/all_gather | solution.py:106
  270.5 51.1 %all-gather.1 = f32[64,64,16]{1,2,0:T(8,128)S(1)} all-gather(f32[1,64,16]{1,2,0:T(8,128)S(1)} %convolution_bitcast_fusion.3), channel_id=2, replica_groups=mesh['rows'=64,'cols'=4] {'rows'}, dimensions={0}, use_global_device_ids=true | all-gather | bytes 266240 | tf_op jit(solution)/shard_map/all_gather | solution.py:111
  (92 shorter events, 28.1 us)
Async XLA Ops:
  7.2 1.6 slice-start
  7.2 261.7 %all-gather.4.cloned.1.call-start = ((), (), s32[]{:S(2)}) async-start(), calls=%async_computation | async-start | bytes 1310720 | tf_op jit(solution)/shard_map/all_gather | solution.py:106
  8.8 6.0 %copy-start = (f32[8192,16]{0,1:T(8,128)S(1)}, f32[8192,16]{0,1:T(8,128)}, u32[]{:S(2)}) copy-start(f32[8192,16]{0,1:T(8,128)} %param.8) | copy-start | bytes 1572868
  8.8 9.1 %copy-start.6 = (s32[64,4]{0,1:T(4,128)S(1)}, s32[64,4]{0,1:T(4,128)}, u32[]{:S(2)}) copy-start(s32[64,4]{0,1:T(4,128)} %param.11) | copy-start | bytes 3076
  12.7 11.5 %copy-start.5 = (s32[1024]{0:T(1024)S(1)}, s32[1024]{0:T(1024)}, u32[]{:S(2)}) copy-start(s32[1024]{0:T(1024)} %param.14) | copy-start | bytes 12292
  14.8 9.4 %collective-permute-start = (bf16[64,128,16]{1,2,0:T(8,128)(2,1)S(1)}, bf16[64,128,16]{1,2,0:T(8,128)(2,1)S(1)}, u32[]{:S(2)}, u32[]{:S(2)}) collective-permute-start(bf16[64,128,16]{1,2,0:T(8,128)(2,1)S(1)} %copy_bitcast_fusion.2), channel_id=1, source_target_pairs={{0,4},{4,8},{8,12},{12,16},{16,20},{20,24},{24,28},{28,32},{32,36}... | collective-permute-start | bytes 786440 | tf_op jit(solution)/shard_map/ppermute | solution.py:16
  16.5 7.7 %collective-permute-start.1 = (bf16[64,128,16]{1,2,0:T(8,128)(2,1)S(1)}, bf16[64,128,16]{1,2,0:T(8,128)(2,1)S(1)}, u32[]{:S(2)}, u32[]{:S(2)}) collective-permute-start(bf16[64,128,16]{1,2,0:T(8,128)(2,1)S(1)} %copy_bitcast_fusion.2), channel_id=1, source_target_pairs={{4,0},{8,4},{12,8},{16,12},{20,16},{24,20},{28,24},{32,28},{36,32}... | collective-permute-start | bytes 786440 | tf_op jit(solution)/shard_map/ppermute | solution.py:17
  25.2 11.9 %copy-start.4 = (s32[8192]{0:T(1024)S(1)}, s32[8192]{0:T(1024)}, u32[]{:S(2)}) copy-start(s32[8192]{0:T(1024)} %param.13) | copy-start | bytes 98308
  31.0 6.1 %collective-permute-start.2 = (bf16[64,128,16]{1,2,0:T(8,128)(2,1)S(1)}, bf16[64,128,16]{1,2,0:T(8,128)(2,1)S(1)}, u32[]{:S(2)}, u32[]{:S(2)}) collective-permute-start(bf16[64,128,16]{1,2,0:T(8,128)(2,1)S(1)} %copy_bitcast_fusion.1), channel_id=1, source_target_pairs={{0,4},{4,8},{8,12},{12,16},{16,20},{20,24},{24,28},{28,32},{32,36}... | collective-permute-start | bytes 786440 | tf_op jit(solution)/shard_map/ppermute | solution.py:16
  35.7 4.7 %collective-permute-start.3 = (bf16[64,128,16]{1,2,0:T(8,128)(2,1)S(1)}, bf16[64,128,16]{1,2,0:T(8,128)(2,1)S(1)}, u32[]{:S(2)}, u32[]{:S(2)}) collective-permute-start(bf16[64,128,16]{1,2,0:T(8,128)(2,1)S(1)} %copy_bitcast_fusion.1), channel_id=1, source_target_pairs={{4,0},{8,4},{12,8},{16,12},{20,16},{24,20},{28,24},{32,28},{36,32}... | collective-permute-start | bytes 786440 | tf_op jit(solution)/shard_map/ppermute | solution.py:17
  47.0 47.3 %copy-start.1 = (bf16[8,3,128,128]{3,2,1,0:T(8,128)(2,1)S(1)}, bf16[8,3,128,128]{3,2,1,0:T(8,128)(2,1)}, u32[]{:S(2)}) copy-start(bf16[8,3,128,128]{3,2,1,0:T(8,128)(2,1)} %param.12) | copy-start | bytes 2359300
  94.6 8.6 %collective-permute-start.5 = (bf16[1,128,16]{1,2,0:T(8,128)(2,1)S(1)}, bf16[1,128,16]{1,2,0:T(8,128)(2,1)S(1)}, u32[]{:S(2)}, u32[]{:S(2)}) collective-permute-start(bf16[1,128,16]{1,2,0:T(8,128)(2,1)S(1)} %get-tuple-element.19), channel_id=1, source_target_pairs={{4,0},{8,4},{12,8},{16,12},{20,16},{24,20},{28,24},{32,28},{36,32}... | collective-permute-start | bytes 12296 | tf_op jit(solution)/shard_map/ppermute | solution.py:17
  95.9 8.1 %collective-permute-start.4 = (bf16[1,128,16]{1,2,0:T(8,128)(2,1)S(1)}, bf16[1,128,16]{1,2,0:T(8,128)(2,1)S(1)}, u32[]{:S(2)}, u32[]{:S(2)}) collective-permute-start(bf16[1,128,16]{1,2,0:T(8,128)(2,1)S(1)} %get-tuple-element.18), channel_id=1, source_target_pairs={{0,4},{4,8},{8,12},{12,16},{16,20},{20,24},{24,28},{28,32},{32,36}... | collective-permute-start | bytes 12296 | tf_op jit(solution)/shard_map/ppermute | solution.py:16
  104.5 5.5 %collective-permute-start.7 = (bf16[1,128,16]{1,2,0:T(8,128)(2,1)S(1)}, bf16[1,128,16]{1,2,0:T(8,128)(2,1)S(1)}, u32[]{:S(2)}, u32[]{:S(2)}) collective-permute-start(bf16[1,128,16]{1,2,0:T(8,128)(2,1)S(1)} %get-tuple-element.17), channel_id=1, source_target_pairs={{4,0},{8,4},{12,8},{16,12},{20,16},{24,20},{28,24},{32,28},{36,32}... | collective-permute-start | bytes 12296 | tf_op jit(solution)/shard_map/ppermute | solution.py:17
  105.8 5.0 %collective-permute-start.6 = (bf16[1,128,16]{1,2,0:T(8,128)(2,1)S(1)}, bf16[1,128,16]{1,2,0:T(8,128)(2,1)S(1)}, u32[]{:S(2)}, u32[]{:S(2)}) collective-permute-start(bf16[1,128,16]{1,2,0:T(8,128)(2,1)S(1)} %get-tuple-element.16), channel_id=1, source_target_pairs={{0,4},{4,8},{8,12},{12,16},{16,20},{20,24},{24,28},{28,32},{32,36}... | collective-permute-start | bytes 12296 | tf_op jit(solution)/shard_map/ppermute | solution.py:16
  118.6 68.6 %copy-start.2 = (f32[128,8192]{1,0:T(8,128)S(1)}, f32[128,8192]{1,0:T(8,128)}, u32[]{:S(2)}) copy-start(f32[128,8192]{1,0:T(8,128)} %param.15) | copy-start | bytes 12582916
  118.6 3.4 %collective-permute-start.8 = (f32[128,16]{1,0:T(8,128)S(1)}, f32[128,16]{1,0:T(8,128)S(1)}, u32[]{:S(2)}, u32[]{:S(2)}) collective-permute-start(f32[128,16]{1,0:T(8,128)S(1)} %slice_select_fusion), channel_id=1, source_target_pairs={{0,4},{4,0},{8,12},{12,8},{16,20},{20,16},{24,28},{28,24},{32,36},... | collective-permute-start | bytes 24584 | tf_op jit(solution)/shard_map/ppermute | solution.py:25
  193.8 1.2 collective-permute-start.9
  198.4 4.4 %collective-permute-start.11 = (bf16[1,128,16]{1,2,0:T(8,128)(2,1)S(1)}, bf16[1,128,16]{1,2,0:T(8,128)(2,1)S(1)}, u32[]{:S(2)}, u32[]{:S(2)}) collective-permute-start(bf16[1,128,16]{1,2,0:T(8,128)(2,1)S(1)} %get-tuple-element.15), channel_id=1, source_target_pairs={{4,0},{8,4},{12,8},{16,12},{20,16},{24,20},{28,24},{32,28},{36,32}... | collective-permute-start | bytes 12296 | tf_op jit(solution)/shard_map/ppermute | solution.py:17
  199.7 3.8 %collective-permute-start.10 = (bf16[1,128,16]{1,2,0:T(8,128)(2,1)S(1)}, bf16[1,128,16]{1,2,0:T(8,128)(2,1)S(1)}, u32[]{:S(2)}, u32[]{:S(2)}) collective-permute-start(bf16[1,128,16]{1,2,0:T(8,128)(2,1)S(1)} %get-tuple-element.14), channel_id=1, source_target_pairs={{0,4},{4,8},{8,12},{12,16},{16,20},{20,24},{24,28},{28,32},{32,36}... | collective-permute-start | bytes 12296 | tf_op jit(solution)/shard_map/ppermute | solution.py:16
  234.8 5.0 %collective-permute-start.12 = (bf16[64,128,16]{1,2,0:T(8,128)(2,1)S(1)}, bf16[64,128,16]{1,2,0:T(8,128)(2,1)S(1)}, u32[]{:S(2)}, u32[]{:S(2)}) collective-permute-start(bf16[64,128,16]{1,2,0:T(8,128)(2,1)S(1)} %copy_bitcast_fusion), channel_id=1, source_target_pairs={{0,4},{4,8},{8,12},{12,16},{16,20},{20,24},{24,28},{28,32},{32,36}... | collective-permute-start | bytes 786440 | tf_op jit(solution)/shard_map/ppermute | solution.py:16
  238.3 5.2 %collective-permute-start.13 = (bf16[64,128,16]{1,2,0:T(8,128)(2,1)S(1)}, bf16[64,128,16]{1,2,0:T(8,128)(2,1)S(1)}, u32[]{:S(2)}, u32[]{:S(2)}) collective-permute-start(bf16[64,128,16]{1,2,0:T(8,128)(2,1)S(1)} %copy_bitcast_fusion), channel_id=1, source_target_pairs={{4,0},{8,4},{12,8},{16,12},{20,16},{24,20},{28,24},{32,28},{36,32}... | collective-permute-start | bytes 786440 | tf_op jit(solution)/shard_map/ppermute | solution.py:17
  250.3 72.0 %copy-start.3 = (f32[8192,16]{0,1:T(8,128)}, f32[8192,16]{0,1:T(8,128)S(1)}, u32[]{:S(2)}) copy-start(f32[8192,16]{0,1:T(8,128)S(1)} %fusion.7) | copy-start | bytes 1572868
Sparse Core Ops, SparseCore 0:
  239.9 28.9 all-gather.3
